TPU v7x, 256 devices: a whole 4x4x8 slice. The times are simulated.
256 devices in a mesh: req: 64 (over y, z, core), rep: 4 (over x).
Axes of the slice: x: 4, y: 4, z: 8, core: 2. Of those that a mesh axis runs over, the one named last changes fastest.
Arguments:
- hidden: bfloat16 [512, 64, 1152], P('rep', 'req'), may hold values from -6 to 6
- norm_gain: float32 [1152], replicated, may hold values from 0.1 to 1.9
- w_qkv: bfloat16 [1152, 1920], replicated, may hold values from -0.1875 to 0.1875
- w_out: bfloat16 [1152, 1152], replicated, may hold values from -0.1875 to 0.1875
- ffn_gain: float32 [1152], replicated, may hold values from 0.1 to 1.9
- w_gate: bfloat16 [1152, 1536], P(None, 'rep'), may hold values from -0.1875 to 0.1875
- w_up: bfloat16 [1152, 1536], P(None, 'rep'), may hold values from -0.1875 to 0.1875
- w_down: bfloat16 [1536, 1152], P('rep'), may hold values from -0.15625 to 0.15625
- cache: bfloat16 [4096, 2, 128, 384], P(('req', 'rep')), may hold values from -363 to 363, as said below
- page_table: int32 [512, 4, 5], P('req', 'rep'), may hold values from 0 to 15, as said below
- cache_len: int32 [512], P('req'), may hold values from 2049 to 2560, as said below
- parents: int32 [512, 64], P('req'), may hold values from 0 to 62, as said below
- accept_leaf: int32 [512], P('req'), may hold values from 0 to 63, as said below
- page_slot: int32 [512], P('req'), may hold values from 0 to 7, as said below
Outputs:
- out: bfloat16 [512, 64, 1152], P('rep', 'req')
- new_pages: bfloat16 [512, 2, 8, 384], P(('req', 'rep'))
Inputs may be any that keep to these rules, and one draw needn't show every extreme that they name: `cache`: no structure is promised. page_table[r, j, s] is the index, among the 16 pages of device j of request r's owner, of the request's logical page s * 4 + j; requests of one owner in aligned blocks of 4 share the pages of logical pages below 16; all other pages are distinct. `cache_len`: every owner holds a request of the largest length. parents[r, 0] = 0; node t >= 1 has depth (t * 7 + 62) // 63 and its parent is a node of the depth before. accept_leaf names a node of depth 8 - 1. `page_slot`: the 8 requests of each owner take each slot once.
All inputs are finite; a program needn't handle non-finite values.
Results may differ from a plain program's by a relative error of at most 0.019.
The roundings to bfloat16 on the way count: a program that leaves them out, or rounds other values in their place, can miss the bound.
Values may be sent and summed in bfloat16 or wider, within the bound.
A program may use at most 128 MiB of HBM per device.

v0:
```python
import jax
import jax.numpy as jnp
from jax import lax
from jax.sharding import PartitionSpec as P

QUERY_HEADS = 18
KEY_VALUE_HEADS = 6
ACC = 8
SCALE = 0.125
EPSILON = 1e-05
THETA = 10000.0


def apply_rotation(values, token_positions, head_count):
    head_columns = values.shape[-1] // head_count
    half_width = head_columns // 2
    shaped = values.reshape(values.shape[:-1] + (head_count, head_columns))
    frequency = THETA ** (-jnp.arange(half_width, dtype=jnp.float32) / half_width)
    angles = token_positions.astype(jnp.float32)[..., None] * frequency
    cosine = jnp.cos(angles)[..., None, :]
    sines = jnp.sin(angles)[..., None, :]
    front_half = shaped[..., :half_width]
    back_half = shaped[..., half_width:]
    turned = jnp.concatenate(
        [front_half * cosine - back_half * sines, back_half * cosine + front_half * sines], axis=-1
    )
    return turned.reshape(values.shape)


def ancestors(parents):
    tree_length = parents.shape[-1]
    identity = jnp.eye(tree_length, dtype=jnp.float32)
    linked = jax.nn.one_hot(parents, tree_length, dtype=jnp.float32)
    reached = jnp.minimum(identity + linked, 1.0)
    for doubling in range(tree_length.bit_length()):
        reached = jnp.minimum(
            jnp.einsum("rts,rsu->rtu", reached, reached, precision=lax.Precision.HIGHEST), 1.0
        )
    return reached


def rms_scaled(values_in, gain):
    scaling = lax.rsqrt(jnp.mean(values_in * values_in, axis=-1, keepdims=True) + EPSILON)
    return (values_in * scaling * gain).astype(jnp.bfloat16)


def project(hidden, norm_gain, w_qkv):
    normed = rms_scaled(hidden.astype(jnp.float32), norm_gain)
    product = jnp.dot(
        normed.reshape(-1, hidden.shape[-1]), w_qkv, preferred_element_type=jnp.float32
    )
    return product.astype(jnp.bfloat16).reshape(hidden.shape[:-1] + (w_qkv.shape[1],))


def attend_part(query_matrix, key_matrix, value_matrix, allowed):
    tree_length = query_matrix.shape[0]
    head_columns = key_matrix.shape[-1]
    grouped_queries = query_matrix.reshape(
        tree_length, KEY_VALUE_HEADS, QUERY_HEADS // KEY_VALUE_HEADS, head_columns
    )
    scores = (
        jnp.einsum(
            "tgrd,sgd->gtrs", grouped_queries, key_matrix, preferred_element_type=jnp.float32
        )
        * SCALE
    )
    scores = jnp.where(allowed[None, :, None, :], scores, -jnp.inf)
    peaks = jnp.max(scores, axis=-1)
    weights = jnp.exp(scores - peaks[..., None])
    totals = jnp.sum(weights, axis=-1)
    summed = jnp.einsum(
        "gtrs,sgd->tgrd",
        weights.astype(jnp.bfloat16),
        value_matrix,
        preferred_element_type=jnp.float32,
    )
    peaks = jnp.transpose(peaks, (1, 0, 2)).reshape(tree_length, QUERY_HEADS)
    totals = jnp.transpose(totals, (1, 0, 2)).reshape(tree_length, QUERY_HEADS)
    return (peaks, totals, summed.reshape(tree_length, QUERY_HEADS * head_columns))


def join_parts(front_part, back_part):
    highest = jnp.maximum(front_part[0], back_part[0])
    front_scale = jnp.exp(front_part[0] - highest)
    back_scale = jnp.exp(back_part[0] - highest)
    totals = front_part[1] * front_scale + back_part[1] * back_scale
    shape_sum = front_part[2].shape
    split_shape = shape_sum[:-1] + (QUERY_HEADS, -1)
    summed = (
        front_part[2].reshape(split_shape) * front_scale[..., None]
        + back_part[2].reshape(split_shape) * back_scale[..., None]
    )
    return (highest, totals, summed.reshape(shape_sum))


def owner_partials(
    queries_all, local_key_rows, local_value_rows, own_reach, cache, page_list, cache_len, own_start
):
    rep_index = lax.axis_index("rep")
    rep_count = lax.axis_size("rep")
    requests = queries_all.shape[0]
    tree_length = queries_all.shape[1]
    owner_page_count = local_key_rows.shape[0]
    slots_count = page_list.shape[1]
    page_length = cache.shape[2]
    head_columns = local_key_rows.shape[-1] // KEY_VALUE_HEADS
    logical = (
        jnp.arange(slots_count, dtype=jnp.int32)[:, None] * rep_count + rep_index
    ) * page_length + jnp.arange(page_length, dtype=jnp.int32)[None, :]
    logical = logical.reshape(slots_count * page_length)

    def per_request(request_item):
        query_matrix, page_ids, cache_end = request_item
        collected_pages = cache[page_ids]
        key_matrix = collected_pages[:, 0].reshape(
            slots_count * page_length, KEY_VALUE_HEADS, head_columns
        )
        value_matrix = collected_pages[:, 1].reshape(
            slots_count * page_length, KEY_VALUE_HEADS, head_columns
        )
        visible = jnp.broadcast_to(
            (logical < cache_end)[None, :], (tree_length, slots_count * page_length)
        )
        return attend_part(query_matrix, key_matrix, value_matrix, visible)

    cached = lax.map(per_request, (queries_all, page_list, cache_len))
    own_queries = lax.dynamic_slice_in_dim(queries_all, own_start, owner_page_count, 0)
    drafted = jax.vmap(attend_part)(
        own_queries,
        local_key_rows.reshape(owner_page_count, tree_length, KEY_VALUE_HEADS, head_columns),
        local_value_rows.reshape(owner_page_count, tree_length, KEY_VALUE_HEADS, head_columns),
        own_reach > 0.5,
    )
    blanks = (
        jnp.full((requests, tree_length, QUERY_HEADS), -jnp.inf, jnp.float32),
        jnp.zeros((requests, tree_length, QUERY_HEADS), jnp.float32),
        jnp.zeros((requests, tree_length, queries_all.shape[2]), jnp.float32),
    )
    placed = tuple(
        (
            lax.dynamic_update_slice_in_dim(blank_part, drafted_part, own_start, 0)
            for blank_part, drafted_part in zip(blanks, drafted)
        )
    )
    return join_parts(cached, placed)


def path_rows(key_matrix, value_matrix, reached, depths, leaf_ids):
    tree_length = reached.shape[-1]
    leaf_hot = jax.nn.one_hot(leaf_ids, tree_length, dtype=jnp.float32)
    on_path = jnp.einsum("rt,rts->rs", leaf_hot, reached, precision=lax.Precision.HIGHEST)
    level_hot = (depths[:, None, :] == jnp.arange(ACC, dtype=jnp.int32)[None, :, None]).astype(
        jnp.float32
    )
    selector = (on_path[:, None, :] * level_hot).astype(jnp.bfloat16)
    stacked = jnp.stack([key_matrix, value_matrix], axis=1)
    return jnp.einsum(
        "ras,rbsc->rbac", selector, stacked, preferred_element_type=jnp.float32
    ).astype(jnp.bfloat16)


def place_rows(rows, page_slot, own_start, owner_page_count):
    slot_ids = own_start + jnp.arange(owner_page_count, dtype=jnp.int32)
    chooser = (page_slot[None, :] == slot_ids[:, None]).astype(jnp.bfloat16)
    return jnp.einsum("pr,rbac->pbac", chooser, rows, preferred_element_type=jnp.float32).astype(
        jnp.bfloat16
    )


def scale_sums(peaks, peak_all, totals, summed):
    factors = jnp.exp(peaks - peak_all)
    split_shape = summed.shape[:-1] + (QUERY_HEADS, -1)
    scaled = (summed.reshape(split_shape) * factors[..., None]).reshape(summed.shape)
    return (scaled, totals * factors)


def body(
    hidden,
    norm_gain,
    w_qkv,
    w_out,
    ffn_gain,
    w_gate,
    w_up,
    w_down,
    cache,
    page_table,
    cache_len,
    parents,
    accept_leaf,
    page_slot,
):
    block_rows, draft_part, model_width = hidden.shape
    channels = w_qkv.shape[1]
    query_columns = w_out.shape[0]
    key_value_columns = (channels - query_columns) // 2
    req_count = lax.axis_size("req")
    rep_count = lax.axis_size("rep")
    rep_index = lax.axis_index("rep")
    requests = cache_len.shape[0]
    owner_page_count = requests // rep_count
    tree_length = parents.shape[1]
    own_start = rep_index * owner_page_count
    projected_rows = project(hidden, norm_gain, w_qkv)
    reached = ancestors(parents)
    depths = jnp.sum(reached, axis=-1).astype(jnp.int32) - 1
    token_positions = cache_len[:, None] + depths
    page_list = page_table[:, 0, :]
    own_reach = lax.dynamic_slice_in_dim(reached, own_start, owner_page_count, 0)
    fanned = lax.all_gather(projected_rows, "rep", axis=0, tiled=True)
    arranged = fanned.reshape(requests, req_count, draft_part, channels)
    owned_pages = lax.all_to_all(arranged, "req", split_axis=1, concat_axis=2, tiled=True).reshape(
        requests, tree_length, channels
    )
    queries_all = apply_rotation(
        owned_pages[..., :query_columns].astype(jnp.float32), token_positions, QUERY_HEADS
    ).astype(jnp.bfloat16)
    keys_all = apply_rotation(
        owned_pages[..., query_columns : query_columns + key_value_columns].astype(jnp.float32),
        token_positions,
        KEY_VALUE_HEADS,
    ).astype(jnp.bfloat16)
    values_all = owned_pages[..., query_columns + key_value_columns :]
    local_key_rows = lax.dynamic_slice_in_dim(keys_all, own_start, owner_page_count, 0)
    local_value_rows = lax.dynamic_slice_in_dim(values_all, own_start, owner_page_count, 0)
    peaks, totals, summed = owner_partials(
        queries_all,
        local_key_rows,
        local_value_rows,
        own_reach,
        cache,
        page_list,
        cache_len,
        own_start,
    )
    returned = (
        lax.all_to_all(
            peaks.reshape(requests, 1, tree_length, QUERY_HEADS),
            "req",
            split_axis=2,
            concat_axis=1,
            tiled=True,
        ),
        lax.all_to_all(
            totals.reshape(requests, 1, tree_length, QUERY_HEADS),
            "req",
            split_axis=2,
            concat_axis=1,
            tiled=True,
        ),
        lax.all_to_all(
            summed.reshape(requests, 1, tree_length, query_columns),
            "req",
            split_axis=2,
            concat_axis=1,
            tiled=True,
        ),
    )
    back_peaks = returned[0].reshape(requests * req_count, draft_part, QUERY_HEADS)
    back_totals = returned[1].reshape(requests * req_count, draft_part, QUERY_HEADS)
    back_sums = returned[2].reshape(requests * req_count, draft_part, query_columns)
    peak_all = lax.pmax(back_peaks, "rep")
    scaled, scaled_totals = scale_sums(back_peaks, peak_all, back_totals, back_sums)
    shared = (
        lax.psum_scatter(scaled, "rep", scatter_dimension=0, tiled=True),
        lax.psum_scatter(scaled_totals, "rep", scatter_dimension=0, tiled=True),
    )
    attended = (
        (shared[0].reshape(block_rows, draft_part, QUERY_HEADS, -1) / shared[1][..., None])
        .reshape(block_rows, draft_part, query_columns)
        .astype(jnp.bfloat16)
    )
    all_rows = path_rows(keys_all, values_all, reached, depths, accept_leaf)
    mixed = jnp.dot(attended.reshape(-1, query_columns), w_out, preferred_element_type=jnp.float32)
    residual = (mixed + hidden.reshape(-1, model_width).astype(jnp.float32)).astype(jnp.bfloat16)
    residual_wide = residual.astype(jnp.float32)
    ffn_in = rms_scaled(residual_wide, ffn_gain).reshape(hidden.shape)
    collected_pages = lax.all_gather(ffn_in, "rep", axis=0, tiled=True)
    rows_in = collected_pages.reshape(-1, model_width)
    gate = jnp.dot(rows_in, w_gate, preferred_element_type=jnp.float32)
    up = jnp.dot(rows_in, w_up, preferred_element_type=jnp.float32)
    activated = (jax.nn.silu(gate) * up).astype(jnp.bfloat16)
    ffn_sum = lax.psum_scatter(
        jnp.dot(activated, w_down, preferred_element_type=jnp.float32).reshape(
            block_rows * lax.axis_size("rep"), draft_part, model_width
        ),
        "rep",
        scatter_dimension=0,
        tiled=True,
    )
    out = (ffn_sum + residual_wide.reshape(hidden.shape)).astype(jnp.bfloat16)
    new_pages = place_rows(all_rows, page_slot, own_start, owner_page_count)
    return (out, new_pages)


def solution(mesh):
    placed = (
        P("rep", "req", None),
        P(),
        P(),
        P(),
        P(),
        P(None, "rep"),
        P(None, "rep"),
        P("rep", None),
        P(("req", "rep"), None, None, None),
        P("req", "rep", None),
        P("req"),
        P("req", None),
        P("req"),
        P("req"),
    )
    return jax.shard_map(
        body,
        mesh=mesh,
        in_specs=placed,
        out_specs=(P("rep", "req", None), P(("req", "rep"), None, None, None)),
        check_vma=False,
    )
```

profile of v0, /device:TPU:1, one launch (start us, length us, event | category | flops | bytes accessed | tf_op | source)
XLA Modules:
  0.0 617.9 jit_solution(11852952766045524678)
XLA Ops:
  8.5 4.1 convolution_convert_fusion
  12.6 36.0 %all-gather.5.cloned.1.call-done = bf16[512,1920]{1,0:T(8,128)(2,1)} async-done(((bf16[128,1920]{1,0:T(8,128)(2,1)}), bf16[512,1920]{1,0:T(8,128)(2,1)}) %all-gather.5.cloned.1.call-update) | async-done | bytes 1966096 | tf_op jit(solution)/shard_map/all_gather | solution.py:210
  48.6 4.0 copy.113
  52.5 11.8 %all-to-all-start = ((bf16[8,64,1,1920]{3,0,2,1:T(8,128)(2,1)}), bf16[8,64,1,1920]{3,0,2,1:T(8,128)(2,1)}, u32[]{:S(2)}, u32[]{:S(2)}) async-start(bf16[8,64,1,1920]{3,0,2,1:T(8,128)(2,1)} %copy.113), calls=%async_computation | async-start | bytes 3932160 | tf_op jit(solution)/shard_map/all_to_all | solution.py:212
  71.9 40.4 %all-to-all-done = bf16[8,64,1,1920]{3,0,2,1:T(8,128)(2,1)} async-done(((bf16[8,64,1,1920]{3,0,2,1:T(8,128)(2,1)}), bf16[8,64,1,1920]{3,0,2,1:T(8,128)(2,1)}, u32[]{:S(2)}, u32[]{:S(2)}) %all-to-all-start) | async-done | bytes 1966112 | tf_op jit(solution)/shard_map/all_to_all | solution.py:212
  125.6 5.5 reshape.319
  131.1 6.6 %subtract_convert_fusion = (bf16[8,64,18,32]{3,2,1,0:T(8,128)(2,1)S(1)}, bf16[8,64,18,32]{3,2,1,0:T(8,128)(2,1)S(1)}) fusion(f32[8,64,18,64]{3,2,1,0:T(8,128)} %reshape.319, f32[8,64,32]{2,1,0:T(8,128)S(1)} %copy-done.3, f32[8,64,32]{2,1,0:T(8,128)S(1)} %copy-done.2), kind=kLoop, calls=%fused_computation.28 | loop fusion | flops 2359296 | bytes 3670016 | tf_op jit(solution)/shard_map/convert.3
  141.2 4.7 convert_element_type.116
  157.6 225.7 %while.15 = (s32[]{:T(128)}, f32[8,64,18]{1,0,2:T(8,128)}, f32[8,64,18]{1,0,2:T(8,128)}, f32[8,64,1152]{2,1,0:T(8,128)}, s32[8]{0:T(128)}, /*index=5*/bf16[8,64,...) while((s32[]{:T(128)}, f32[8,64,18]{1,0,2:T(8,128)}, ...), condition=%wide.region_5.6_spmd.clone, body=%wide.region_2.5_spmd.clone.sunk | while | flops 196853776 | bytes 19970600 | solution.py:126
  387.7 6.1 all-to-all-start.2
  400.1 5.3 mul.245
  405.5 3.8 mul.248
  409.3 5.3 mul.249
  415.7 10.6 %all-to-all-start.3 = ((f32[64,1,144]{2,1,0:T(1,128)}), f32[64,1,144]{2,1,0:T(1,128)S(1)}, u32[]{:S(2)}, u32[]{:S(2)}) async-start(f32[64,1,144]{2,1,0:T(1,128)} %reshape.357), calls=%async_computation.4 | async-start | bytes 131072 | tf_op jit(solution)/shard_map/all_to_all | solution.py:244
  426.3 4.2 bitcast_add_fusion
  436.0 7.9 %all-to-all-start.1 = ((f32[8,1,64,1152]{3,0,1,2:T(8,128)}), f32[8,1,64,1152]{3,0,1,2:T(8,128)}, u32[]{:S(2)}, u32[]{:S(2)}) async-start(f32[8,1,64,1152]{3,0,1,2:T(8,128)} %copy.132), calls=%async_computation.1 | async-start | bytes 4718592 | tf_op jit(solution)/shard_map/all_to_all | solution.py:251
  446.9 13.3 %pmax.7 = f32[512,1,18]{0,1,2:T(1,128)S(1)} all-reduce(f32[512,1,18]{0,1,2:T(1,128)S(1)} %reshape.309), channel_id=1, replica_groups=mesh['req'=64,'rep'=4] {'rep'}, use_global_device_ids=true, to_apply=%region_7.8 | all-reduce | flops 9216 | bytes 73728 | tf_op jit(solution)/shard_map/pmax | solution.py:262
  465.1 4.1 copy.158
  469.3 5.2 bitcast_reduce_fusion
  474.5 25.9 %all-to-all-done.1 = f32[8,1,64,1152]{3,0,1,2:T(8,128)} async-done(((f32[8,1,64,1152]{3,0,1,2:T(8,128)}), f32[8,1,64,1152]{3,0,1,2:T(8,128)}, u32[]{:S(2)}, u32[]{:S(2)}) %all-to-all-start.1) | async-done | bytes 2359328 | tf_op jit(solution)/shard_map/all_to_all | solution.py:251
  510.0 26.1 %reduce-scatter.6.cloned.1.call-done = f32[128,1,1152]{2,0,1:T(8,128)} async-done(((f32[512,1,1152]{2,0,1:T(8,128)}), f32[128,1,1152]{2,0,1:T(8,128)}) %reduce-scatter.6.cloned.1.call-update) | async-done | bytes 589840 | tf_op jit(solution)/shard_map/reduce_scatter | solution.py:265
  539.1 24.7 %all-gather.7.cloned.1.call-done = bf16[512,1152]{1,0:T(8,128)(2,1)} async-done(((bf16[128,1152]{1,0:T(8,128)(2,1)}), bf16[512,1152]{1,0:T(8,128)(2,1)}) %all-gather.7.cloned.1.call-update) | async-done | bytes 1179664 | tf_op jit(solution)/shard_map/all_gather | solution.py:278
  567.0 5.0 convolution_bitcast_fusion
  577.9 31.4 %reduce-scatter.8.cloned.1.call-done = f32[128,1,1152]{2,0,1:T(8,128)} async-done(((f32[512,1,1152]{2,0,1:T(8,128)}), f32[128,1,1152]{2,0,1:T(8,128)}) %reduce-scatter.8.cloned.1.call-update) | async-done | bytes 589840 | tf_op jit(solution)/shard_map/reduce_scatter | solution.py:283
  (332 shorter events, 310.8 us)
Async XLA Ops:
  7.2 529.0 %copy-start = (bf16[1152,1152]{1,0:T(8,128)(2,1)S(1)}, bf16[1152,1152]{1,0:T(8,128)(2,1)}, u32[]{:S(2)}) copy-start(bf16[1152,1152]{1,0:T(8,128)(2,1)} %param.19) | copy-start | bytes 7962628
  7.2 41.4 %all-gather.5.cloned.1.call-start = ((), (), s32[]{:S(2)}) async-start(), calls=%async_computation.9 | async-start | bytes 2457600 | tf_op jit(solution)/shard_map/all_gather | solution.py:210
  52.5 11.8 %copy-start.16 = (s32[8,64]{1,0:T(8,128)S(1)}, s32[8,64]{1,0:T(8,128)}, u32[]{:S(2)}) copy-start(s32[8,64]{1,0:T(8,128)} %param.27) | copy-start | bytes 6148
  52.5 59.8 %all-to-all-start = ((bf16[8,64,1,1920]{3,0,2,1:T(8,128)(2,1)}), bf16[8,64,1,1920]{3,0,2,1:T(8,128)(2,1)}, u32[]{:S(2)}, u32[]{:S(2)}) async-start(bf16[8,64,1,1920]{3,0,2,1:T(8,128)(2,1)} %copy.113), calls=%async_computation | async-start | bytes 3932160 | tf_op jit(solution)/shard_map/all_to_all | solution.py:212
  157.6 10.0 %copy-start.13 = (s32[8,5]{1,0:T(8,128)}, s32[8,5]{1,0:T(8,128)S(1)}, u32[]{:S(2)}) copy-start(s32[8,5]{1,0:T(8,128)S(1)} %get-tuple-element.250) | copy-start | bytes 484 | tf_op jit(solution)/shard_map/while
  185.8 10.0 %copy-start.13 = (s32[8,5]{1,0:T(8,128)}, s32[8,5]{1,0:T(8,128)S(1)}, u32[]{:S(2)}) copy-start(s32[8,5]{1,0:T(8,128)S(1)} %get-tuple-element.250) | copy-start | bytes 484 | tf_op jit(solution)/shard_map/while
  214.0 10.0 %copy-start.13 = (s32[8,5]{1,0:T(8,128)}, s32[8,5]{1,0:T(8,128)S(1)}, u32[]{:S(2)}) copy-start(s32[8,5]{1,0:T(8,128)S(1)} %get-tuple-element.250) | copy-start | bytes 484 | tf_op jit(solution)/shard_map/while
  242.2 10.0 %copy-start.13 = (s32[8,5]{1,0:T(8,128)}, s32[8,5]{1,0:T(8,128)S(1)}, u32[]{:S(2)}) copy-start(s32[8,5]{1,0:T(8,128)S(1)} %get-tuple-element.250) | copy-start | bytes 484 | tf_op jit(solution)/shard_map/while
  270.4 10.0 %copy-start.13 = (s32[8,5]{1,0:T(8,128)}, s32[8,5]{1,0:T(8,128)S(1)}, u32[]{:S(2)}) copy-start(s32[8,5]{1,0:T(8,128)S(1)} %get-tuple-element.250) | copy-start | bytes 484 | tf_op jit(solution)/shard_map/while
  298.6 10.0 %copy-start.13 = (s32[8,5]{1,0:T(8,128)}, s32[8,5]{1,0:T(8,128)S(1)}, u32[]{:S(2)}) copy-start(s32[8,5]{1,0:T(8,128)S(1)} %get-tuple-element.250) | copy-start | bytes 484 | tf_op jit(solution)/shard_map/while
  326.8 10.0 %copy-start.13 = (s32[8,5]{1,0:T(8,128)}, s32[8,5]{1,0:T(8,128)S(1)}, u32[]{:S(2)}) copy-start(s32[8,5]{1,0:T(8,128)S(1)} %get-tuple-element.250) | copy-start | bytes 484 | tf_op jit(solution)/shard_map/while
  348.6 6.5 %copy-start.14 = (s32[8,5]{1,0:T(8,128)S(1)}, s32[8,5]{1,0:T(8,128)}, u32[]{:S(2)}) copy-start(s32[8,5]{1,0:T(8,128)} %copy-done.13) | copy-start | bytes 484 | tf_op jit(solution)/shard_map/while
  355.0 10.0 %copy-start.13 = (s32[8,5]{1,0:T(8,128)}, s32[8,5]{1,0:T(8,128)S(1)}, u32[]{:S(2)}) copy-start(s32[8,5]{1,0:T(8,128)S(1)} %get-tuple-element.250) | copy-start | bytes 484 | tf_op jit(solution)/shard_map/while
  383.3 12.1 %copy-start.4 = (f32[2,1,64,1152]{3,2,0,1:T(8,128)S(1)}, f32[2,1,64,1152]{3,2,0,1:T(8,128)}, u32[]{:S(2)}) copy-start(f32[2,1,64,1152]{3,2,0,1:T(8,128)} %copy.130) | copy-start | bytes 1769476
  387.7 8.5 %copy-start.10 = (f32[8,64,18]{1,0,2:T(8,128)S(1)}, f32[8,64,18]{1,0,2:T(8,128)}, u32[]{:S(2)}) copy-start(f32[8,64,18]{1,0,2:T(8,128)} %get-tuple-element.133) | copy-start | bytes 110596
  387.7 28.0 %all-to-all-start.2 = ((f32[64,1,144]{2,1,0:T(1,128)}), f32[64,1,144]{2,1,0:T(1,128)S(1)}, u32[]{:S(2)}, u32[]{:S(2)}) async-start(f32[64,1,144]{2,1,0:T(1,128)} %reshape.355), calls=%async_computation.2 | async-start | bytes 131072 | tf_op jit(solution)/shard_map/all_to_all | solution.py:237
  415.7 20.3 %all-to-all-start.3 = ((f32[64,1,144]{2,1,0:T(1,128)}), f32[64,1,144]{2,1,0:T(1,128)S(1)}, u32[]{:S(2)}, u32[]{:S(2)}) async-start(f32[64,1,144]{2,1,0:T(1,128)} %reshape.357), calls=%async_computation.4 | async-start | bytes 131072 | tf_op jit(solution)/shard_map/all_to_all | solution.py:244
  436.0 64.5 %all-to-all-start.1 = ((f32[8,1,64,1152]{3,0,1,2:T(8,128)}), f32[8,1,64,1152]{3,0,1,2:T(8,128)}, u32[]{:S(2)}, u32[]{:S(2)}) async-start(f32[8,1,64,1152]{3,0,1,2:T(8,128)} %copy.132), calls=%async_computation.1 | async-start | bytes 4718592 | tf_op jit(solution)/shard_map/all_to_all | solution.py:251
  443.9 60.7 %reduce-scatter.10.cloned.1.call-start = ((), (), s32[]{:S(2)}) async-start(), calls=%async_computation.11 | async-start | bytes 327680
  474.5 61.7 %reduce-scatter.6.cloned.1.call-start = ((), (), s32[]{:S(2)}) async-start(), calls=%async_computation.7 | async-start | bytes 2949120 | tf_op jit(solution)/shard_map/reduce_scatter | solution.py:265
  504.5 31.7 %copy-start.7 = (bf16[128,1,1152]{2,0,1:T(8,128)(2,1)S(1)}, bf16[128,1,1152]{2,0,1:T(8,128)(2,1)}, u32[]{:S(2)}) copy-start(bf16[128,1,1152]{2,0,1:T(8,128)(2,1)} %param.16) | copy-start | bytes 884740
  504.5 59.3 %all-gather.7.cloned.1.call-start = ((), (), s32[]{:S(2)}) async-start(), calls=%async_computation.10 | async-start | bytes 1474560 | tf_op jit(solution)/shard_map/all_gather | solution.py:278
  510.0 28.1 %copy-start.11 = (f32[1152]{0:T(1024)S(1)}, f32[1152]{0:T(1024)}, u32[]{:S(2)}) copy-start(f32[1152]{0:T(1024)} %param.20) | copy-start | bytes 13828
  539.0 70.2 %reduce-scatter.8.cloned.1.call-start = ((), (), s32[]{:S(2)}) async-start(), calls=%async_computation.8 | async-start | bytes 2949120 | tf_op jit(solution)/shard_map/reduce_scatter | solution.py:283
  (18 other events, 83.5 us)
Sparse Core Ops, SparseCore 0:
  12.7 35.8 all-gather.4
  474.6 23.4 reduce-scatter.9
  504.6 31.5 reduce-scatter.5
  539.1 24.6 all-gather.6
  572.2 37.0 reduce-scatter.7
where the time goes:
time: 625 us; the launch traced here: 618 us
  local copies, waits for them, and re-layouts  229 us (37%)
  waiting for transfers between devices  187 us (30%)
  matrix products  70.4 us (11%)
  other arithmetic  66.2 us (11%)
  starting transfers between devices  36.6 us (6%)
  between operations  14.5 us (2%)
  blocking collectives  13.3 us (2%)
    all_to_all x1, waiting for transfers between devices, body(): lax.all_to_all(arranged, 'req', split_axis=1, concat_axis=2, tiled=True)  40.4 us
    all_gather x1, waiting for transfers between devices, body(): fanned = lax.all_gather(projected_rows, 'rep', axis=0, tiled=True)  36 us
    dynamic_update_slice x32, local copies, waits for them, and re-layouts, owner_partials(): cached = lax.map(per_request, (queries_all, page_list, cache_len))  32.5 us
    reduce_scatter x1, waiting for transfers between devices, body(): lax.psum_scatter(jnp.dot(activated, w_down, preferred_element_type=jnp.fl...  31.4 us
    slice x16, local copies, waits for them, and re-layouts, per_request(): collected_pages[:, 1]  30.2 us
    gather x8, local copies, waits for them, and re-layouts, per_request(): collected_pages = cache[page_ids]  28.7 us
    dot_general x9, matrix products, attend_part(): jnp.einsum('tgrd,sgd->gtrs', grouped_queries, key_matrix, preferred_eleme...  26.9 us
    reduce_scatter x1, waiting for transfers between devices, body(): lax.psum_scatter(scaled, 'rep', scatter_dimension=0, tiled=True)  26.1 us
  transfers between devices with their start and end apart: 9, of which 7 were waited for; matrix products, arithmetic and copies ran while one was open for 11% of the time, Pallas kernels for 0%

commit v1 on v0

--- a/solution.py
+++ b/solution.py
@@ -275,7 +275,9 @@
     residual = (mixed + hidden.reshape(-1, model_width).astype(jnp.float32)).astype(jnp.bfloat16)
     residual_wide = residual.astype(jnp.float32)
     ffn_in = rms_scaled(residual_wide, ffn_gain).reshape(hidden.shape)
-    collected_pages = lax.all_gather(ffn_in, "rep", axis=0, tiled=True)
+    collected_pages = jnp.concatenate(
+        lax.all_to_all(jnp.stack(lax.axis_size("rep") * [ffn_in], axis=0), "rep", 0, 0), axis=0
+    )
     rows_in = collected_pages.reshape(-1, model_width)
     gate = jnp.dot(rows_in, w_gate, preferred_element_type=jnp.float32)
     up = jnp.dot(rows_in, w_up, preferred_element_type=jnp.float32)

time: 625 us -> 616 us (0.986)
  waiting for transfers between devices: 187 us -> 161 us
  blocking collectives: 13.3 us -> 31.6 us
    all_gather x1 -> x0, waiting for transfers between devices: 24.7 us -> none  [body(): collected_pages = lax.all_gather(ffn_in, 'rep', axis=0, tiled=True)]
    all_to_all x0 -> x1, blocking collectives: none -> 18.3 us  [body(): lax.all_to_all(jnp.stack(lax.axis_size('rep') * [ffn_in], axis=0), 'rep',...]
    unnamed x45 -> x49, local copies, waits for them, and re-layouts: 18 us -> 19 us
  transfers between devices with their start and end apart: 9 -> 8, of which waited for: 7 -> 6; matrix products, arithmetic and copies ran while one was open for 11% -> 11% of each run, Pallas kernels for 0% -> 0%
where the time goes in v1:
time: 616 us; the launch traced here: 609 us
  local copies, waits for them, and re-layouts  231 us (38%)
  waiting for transfers between devices  161 us (26%)
  matrix products  68.9 us (11%)
  other arithmetic  65.2 us (11%)
  starting transfers between devices  36.4 us (6%)
  blocking collectives  31.6 us (5%)
  between operations  14.5 us (2%)
    all_to_all x1, waiting for transfers between devices, body(): lax.all_to_all(arranged, 'req', split_axis=1, concat_axis=2, tiled=True)  40.6 us
    all_gather x1, waiting for transfers between devices, body(): fanned = lax.all_gather(projected_rows, 'rep', axis=0, tiled=True)  36 us
    dynamic_update_slice x32, local copies, waits for them, and re-layouts, owner_partials(): cached = lax.map(per_request, (queries_all, page_list, cache_len))  32.6 us
    slice x16, local copies, waits for them, and re-layouts, per_request(): collected_pages[:, 1]  30.2 us
    reduce_scatter x1, waiting for transfers between devices, body(): lax.psum_scatter(jnp.dot(activated, w_down, preferred_element_type=jnp.fl...  29.3 us
    gather x8, local copies, waits for them, and re-layouts, per_request(): collected_pages = cache[page_ids]  28.8 us
    dot_general x9, matrix products, attend_part(): jnp.einsum('tgrd,sgd->gtrs', grouped_queries, key_matrix, preferred_eleme...  27 us
    reduce_scatter x1, waiting for transfers between devices, body(): lax.psum_scatter(scaled, 'rep', scatter_dimension=0, tiled=True)  26.1 us
  transfers between devices with their start and end apart: 8, of which 6 were waited for; matrix products, arithmetic and copies ran while one was open for 11% of the time, Pallas kernels for 0%

profile of v1, /device:TPU:1, one launch (start us, length us, event | category | flops | bytes accessed | tf_op | source)
XLA Modules:
  0.0 608.5 jit_solution(7562464777624329318)
XLA Ops:
  8.5 4.1 convolution_convert_fusion
  12.6 36.0 %all-gather.3.cloned.1.call-done = bf16[512,1920]{1,0:T(8,128)(2,1)} async-done(((bf16[128,1920]{1,0:T(8,128)(2,1)}), bf16[512,1920]{1,0:T(8,128)(2,1)}) %all-gather.3.cloned.1.call-update) | async-done | bytes 1966096 | tf_op jit(solution)/shard_map/all_gather | solution.py:210
  48.6 3.9 copy.113
  52.5 11.6 %all-to-all-start = ((bf16[8,64,1,1920]{3,0,2,1:T(8,128)(2,1)}), bf16[8,64,1,1920]{3,0,2,1:T(8,128)(2,1)}, u32[]{:S(2)}, u32[]{:S(2)}) async-start(bf16[8,64,1,1920]{3,0,2,1:T(8,128)(2,1)} %copy.113), calls=%async_computation | async-start | bytes 3932160 | tf_op jit(solution)/shard_map/all_to_all | solution.py:212
  71.6 40.6 %all-to-all-done = bf16[8,64,1,1920]{3,0,2,1:T(8,128)(2,1)} async-done(((bf16[8,64,1,1920]{3,0,2,1:T(8,128)(2,1)}), bf16[8,64,1,1920]{3,0,2,1:T(8,128)(2,1)}, u32[]{:S(2)}, u32[]{:S(2)}) %all-to-all-start) | async-done | bytes 1966112 | tf_op jit(solution)/shard_map/all_to_all | solution.py:212
  125.4 5.5 reshape.313
  130.9 6.7 %subtract_convert_fusion = (bf16[8,64,18,32]{3,2,1,0:T(8,128)(2,1)S(1)}, bf16[8,64,18,32]{3,2,1,0:T(8,128)(2,1)S(1)}) fusion(f32[8,64,18,64]{3,2,1,0:T(8,128)} %reshape.313, f32[8,64,32]{2,1,0:T(8,128)S(1)} %copy-done.3, f32[8,64,32]{2,1,0:T(8,128)S(1)} %copy-done.2), kind=kLoop, calls=%fused_computation.28 | loop fusion | flops 2359296 | bytes 3670016 | tf_op jit(solution)/shard_map/convert.3
  141.0 5.0 convert_element_type.116
  157.8 225.8 %while.15 = (s32[]{:T(128)}, f32[8,64,18]{1,0,2:T(8,128)}, f32[8,64,18]{1,0,2:T(8,128)}, f32[8,64,1152]{2,1,0:T(8,128)}, s32[8]{0:T(128)}, /*index=5*/bf16[8,64,...) while((s32[]{:T(128)}, f32[8,64,18]{1,0,2:T(8,128)}, ...), condition=%wide.region_5.6_spmd.clone, body=%wide.region_2.5_spmd.clone.sunk | while | flops 196853776 | bytes 19970600 | solution.py:126
  388.0 6.1 all-to-all-start.2
  400.5 5.3 mul.245
  405.9 3.8 mul.248
  409.7 5.3 mul.249
  416.0 10.6 %all-to-all-start.3 = ((f32[64,1,144]{2,1,0:T(1,128)}), f32[64,1,144]{2,1,0:T(1,128)S(1)}, u32[]{:S(2)}, u32[]{:S(2)}) async-start(f32[64,1,144]{2,1,0:T(1,128)} %reshape.349), calls=%async_computation.4 | async-start | bytes 131072 | tf_op jit(solution)/shard_map/all_to_all | solution.py:244
  426.7 4.2 bitcast_add_fusion
  436.3 7.9 %all-to-all-start.1 = ((f32[8,1,64,1152]{3,0,1,2:T(8,128)}), f32[8,1,64,1152]{3,0,1,2:T(8,128)}, u32[]{:S(2)}, u32[]{:S(2)}) async-start(f32[8,1,64,1152]{3,0,1,2:T(8,128)} %copy.132), calls=%async_computation.1 | async-start | bytes 4718592 | tf_op jit(solution)/shard_map/all_to_all | solution.py:251
  447.2 13.3 %pmax.7 = f32[512,1,18]{0,1,2:T(1,128)S(1)} all-reduce(f32[512,1,18]{0,1,2:T(1,128)S(1)} %reshape.305), channel_id=1, replica_groups=mesh['req'=64,'rep'=4] {'rep'}, use_global_device_ids=true, to_apply=%region_7.8 | all-reduce | flops 9216 | bytes 73728 | tf_op jit(solution)/shard_map/pmax | solution.py:262
  465.5 4.1 copy.158
  469.6 5.2 bitcast_reduce_fusion
  474.8 25.9 %all-to-all-done.1 = f32[8,1,64,1152]{3,0,1,2:T(8,128)} async-done(((f32[8,1,64,1152]{3,0,1,2:T(8,128)}), f32[8,1,64,1152]{3,0,1,2:T(8,128)}, u32[]{:S(2)}, u32[]{:S(2)}) %all-to-all-start.1) | async-done | bytes 2359328 | tf_op jit(solution)/shard_map/all_to_all | solution.py:251
  510.4 26.1 %reduce-scatter.6.cloned.1.call-done = f32[128,1,1152]{2,0,1:T(8,128)} async-done(((f32[512,1,1152]{2,0,1:T(8,128)}), f32[128,1,1152]{2,0,1:T(8,128)}) %reduce-scatter.6.cloned.1.call-update) | async-done | bytes 589840 | tf_op jit(solution)/shard_map/reduce_scatter | solution.py:265
  538.7 18.3 %all_to_all.20 = bf16[4,128,1,1152]{3,1,2,0:T(8,128)(2,1)S(1)} all-to-all(bf16[4,128,1,1152]{3,1,2,0:T(8,128)(2,1)S(1)} %stack.10), channel_id=1, replica_groups=mesh['req'=64,'rep'=4] {'rep'}, dimensions={0} | all-to-all | bytes 2359296 | tf_op jit(solution)/shard_map/all_to_all | solution.py:279
  559.7 5.0 convolution_bitcast_fusion
  570.6 29.3 %reduce-scatter.8.cloned.1.call-done = f32[128,1,1152]{2,0,1:T(8,128)} async-done(((f32[512,1,1152]{2,0,1:T(8,128)}), f32[128,1,1152]{2,0,1:T(8,128)}) %reduce-scatter.8.cloned.1.call-update) | async-done | bytes 589840 | tf_op jit(solution)/shard_map/reduce_scatter | solution.py:285
  (335 shorter events, 309.7 us)
Async XLA Ops:
  7.2 529.3 %copy-start = (bf16[1152,1152]{1,0:T(8,128)(2,1)S(1)}, bf16[1152,1152]{1,0:T(8,128)(2,1)}, u32[]{:S(2)}) copy-start(bf16[1152,1152]{1,0:T(8,128)(2,1)} %param.19) | copy-start | bytes 7962628
  7.2 41.4 %all-gather.3.cloned.1.call-start = ((), (), s32[]{:S(2)}) async-start(), calls=%async_computation.10 | async-start | bytes 2457600 | tf_op jit(solution)/shard_map/all_gather | solution.py:210
  52.5 11.7 %copy-start.18 = (s32[8,64]{1,0:T(8,128)S(1)}, s32[8,64]{1,0:T(8,128)}, u32[]{:S(2)}) copy-start(s32[8,64]{1,0:T(8,128)} %param.27) | copy-start | bytes 6148
  52.5 59.7 %all-to-all-start = ((bf16[8,64,1,1920]{3,0,2,1:T(8,128)(2,1)}), bf16[8,64,1,1920]{3,0,2,1:T(8,128)(2,1)}, u32[]{:S(2)}, u32[]{:S(2)}) async-start(bf16[8,64,1,1920]{3,0,2,1:T(8,128)(2,1)} %copy.113), calls=%async_computation | async-start | bytes 3932160 | tf_op jit(solution)/shard_map/all_to_all | solution.py:212
  157.8 10.1 %copy-start.14 = (s32[8,5]{1,0:T(8,128)}, s32[8,5]{1,0:T(8,128)S(1)}, u32[]{:S(2)}) copy-start(s32[8,5]{1,0:T(8,128)S(1)} %get-tuple-element.250) | copy-start | bytes 484 | tf_op jit(solution)/shard_map/while
  186.0 10.1 %copy-start.14 = (s32[8,5]{1,0:T(8,128)}, s32[8,5]{1,0:T(8,128)S(1)}, u32[]{:S(2)}) copy-start(s32[8,5]{1,0:T(8,128)S(1)} %get-tuple-element.250) | copy-start | bytes 484 | tf_op jit(solution)/shard_map/while
  214.3 10.1 %copy-start.14 = (s32[8,5]{1,0:T(8,128)}, s32[8,5]{1,0:T(8,128)S(1)}, u32[]{:S(2)}) copy-start(s32[8,5]{1,0:T(8,128)S(1)} %get-tuple-element.250) | copy-start | bytes 484 | tf_op jit(solution)/shard_map/while
  242.5 10.1 %copy-start.14 = (s32[8,5]{1,0:T(8,128)}, s32[8,5]{1,0:T(8,128)S(1)}, u32[]{:S(2)}) copy-start(s32[8,5]{1,0:T(8,128)S(1)} %get-tuple-element.250) | copy-start | bytes 484 | tf_op jit(solution)/shard_map/while
  270.7 10.1 %copy-start.14 = (s32[8,5]{1,0:T(8,128)}, s32[8,5]{1,0:T(8,128)S(1)}, u32[]{:S(2)}) copy-start(s32[8,5]{1,0:T(8,128)S(1)} %get-tuple-element.250) | copy-start | bytes 484 | tf_op jit(solution)/shard_map/while
  298.9 10.1 %copy-start.14 = (s32[8,5]{1,0:T(8,128)}, s32[8,5]{1,0:T(8,128)S(1)}, u32[]{:S(2)}) copy-start(s32[8,5]{1,0:T(8,128)S(1)} %get-tuple-element.250) | copy-start | bytes 484 | tf_op jit(solution)/shard_map/while
  327.1 10.1 %copy-start.14 = (s32[8,5]{1,0:T(8,128)}, s32[8,5]{1,0:T(8,128)S(1)}, u32[]{:S(2)}) copy-start(s32[8,5]{1,0:T(8,128)S(1)} %get-tuple-element.250) | copy-start | bytes 484 | tf_op jit(solution)/shard_map/while
  348.9 6.5 %copy-start.15 = (s32[8,5]{1,0:T(8,128)S(1)}, s32[8,5]{1,0:T(8,128)}, u32[]{:S(2)}) copy-start(s32[8,5]{1,0:T(8,128)} %copy-done.14) | copy-start | bytes 484 | tf_op jit(solution)/shard_map/while
  355.4 10.1 %copy-start.14 = (s32[8,5]{1,0:T(8,128)}, s32[8,5]{1,0:T(8,128)S(1)}, u32[]{:S(2)}) copy-start(s32[8,5]{1,0:T(8,128)S(1)} %get-tuple-element.250) | copy-start | bytes 484 | tf_op jit(solution)/shard_map/while
  383.6 12.1 %copy-start.4 = (f32[2,1,64,1152]{3,2,0,1:T(8,128)S(1)}, f32[2,1,64,1152]{3,2,0,1:T(8,128)}, u32[]{:S(2)}) copy-start(f32[2,1,64,1152]{3,2,0,1:T(8,128)} %copy.130) | copy-start | bytes 1769476
  388.0 8.5 %copy-start.11 = (f32[8,64,18]{1,0,2:T(8,128)S(1)}, f32[8,64,18]{1,0,2:T(8,128)}, u32[]{:S(2)}) copy-start(f32[8,64,18]{1,0,2:T(8,128)} %get-tuple-element.133) | copy-start | bytes 110596
  388.0 28.0 %all-to-all-start.2 = ((f32[64,1,144]{2,1,0:T(1,128)}), f32[64,1,144]{2,1,0:T(1,128)S(1)}, u32[]{:S(2)}, u32[]{:S(2)}) async-start(f32[64,1,144]{2,1,0:T(1,128)} %reshape.347), calls=%async_computation.2 | async-start | bytes 131072 | tf_op jit(solution)/shard_map/all_to_all | solution.py:237
  416.0 20.2 %all-to-all-start.3 = ((f32[64,1,144]{2,1,0:T(1,128)}), f32[64,1,144]{2,1,0:T(1,128)S(1)}, u32[]{:S(2)}, u32[]{:S(2)}) async-start(f32[64,1,144]{2,1,0:T(1,128)} %reshape.349), calls=%async_computation.4 | async-start | bytes 131072 | tf_op jit(solution)/shard_map/all_to_all | solution.py:244
  436.3 64.5 %all-to-all-start.1 = ((f32[8,1,64,1152]{3,0,1,2:T(8,128)}), f32[8,1,64,1152]{3,0,1,2:T(8,128)}, u32[]{:S(2)}, u32[]{:S(2)}) async-start(f32[8,1,64,1152]{3,0,1,2:T(8,128)} %copy.132), calls=%async_computation.1 | async-start | bytes 4718592 | tf_op jit(solution)/shard_map/all_to_all | solution.py:251
  444.2 60.7 %reduce-scatter.10.cloned.1.call-start = ((), (), s32[]{:S(2)}) async-start(), calls=%async_computation.11 | async-start | bytes 327680
  474.8 61.7 %reduce-scatter.6.cloned.1.call-start = ((), (), s32[]{:S(2)}) async-start(), calls=%async_computation.8 | async-start | bytes 2949120 | tf_op jit(solution)/shard_map/reduce_scatter | solution.py:265
  504.8 31.7 %copy-start.8 = (bf16[128,1,1152]{2,0,1:T(8,128)(2,1)S(1)}, bf16[128,1,1152]{2,0,1:T(8,128)(2,1)}, u32[]{:S(2)}) copy-start(bf16[128,1,1152]{2,0,1:T(8,128)(2,1)} %param.16) | copy-start | bytes 884740
  504.8 95.1 %reduce-scatter.8.cloned.1.call-start = ((), (), s32[]{:S(2)}) async-start(), calls=%async_computation.9 | async-start | bytes 2949120 | tf_op jit(solution)/shard_map/reduce_scatter | solution.py:285
  510.4 28.1 %copy-start.12 = (f32[1152]{0:T(1024)S(1)}, f32[1152]{0:T(1024)}, u32[]{:S(2)}) copy-start(f32[1152]{0:T(1024)} %param.20) | copy-start | bytes 13828
  538.5 19.6 %copy-start.17 = (bf16[1152,384]{1,0:T(8,128)(2,1)S(1)}, bf16[1152,384]{1,0:T(8,128)(2,1)}, u32[]{:S(2)}) copy-start(bf16[1152,384]{1,0:T(8,128)(2,1)} %param.21) | copy-start | bytes 2654212
  (19 other events, 84.6 us)
Sparse Core Ops, SparseCore 0:
  12.7 35.8 all-gather.2
  474.9 23.4 reduce-scatter.9
  504.9 31.5 reduce-scatter.5
  564.9 35.0 reduce-scatter.7
